TPU v7x, 32 devices: a whole 2x2x4 slice. The times are simulated.
32 devices in a mesh: clip: 8 (over y, x, core), shard: 4 (over z).
Axes of the slice: x: 2, y: 2, z: 4, core: 2. Of those that a mesh axis runs over, the one named last changes fastest.
Arguments:
- tokens: bfloat16 [8, 9216, 768], P('clip', 'shard'), may hold values from -6 to 6
- scales: float32 [8, 6, 9216], P('clip', None, 'shard'), may hold values from 0.1875 to 5
- slot_params: bfloat16 [768, 128], replicated, may hold values from -2 to 2
- expand_weight: bfloat16 [64, 768, 3072], P(('clip', 'shard')), may hold values from -0.21875 to 0.21875
- expand_bias: bfloat16 [64, 3072], P(('clip', 'shard')), may hold values from -4 to 4
- reduce_weight: bfloat16 [64, 3072, 768], P(('clip', 'shard')), may hold values from -0.109375 to 0.109375
- reduce_bias: bfloat16 [64, 768], P(('clip', 'shard')), may hold values from -4 to 4
Outputs:
- mixed: bfloat16 [8, 9216, 768], P('clip', 'shard')
All inputs are finite; a program needn't handle non-finite values.
Results may differ from a plain program's by a relative error of at most 0.012.
The roundings to bfloat16 on the way count: a program that leaves them out, or rounds other values in their place, can miss the bound.
Values may be sent and summed in bfloat16 or wider, within the bound.
A program may use at most 128 MiB of HBM per device.

v0:
```python
import jax
import jax.numpy as jnp
from jax import lax
from jax.sharding import PartitionSpec as P


def expert_apply(slot_inputs, expand_weight, expand_bias, reduce_weight, reduce_bias):
    widened = slot_inputs.astype(jnp.float32)
    normalized = (
        widened * lax.rsqrt(jnp.mean(widened * widened, axis=-1, keepdims=True) + 1e-06)
    ).astype(jnp.bfloat16)
    hidden = jnp.einsum(
        "cisd,idf->cisf", normalized, expand_weight, preferred_element_type=jnp.float32
    )
    hidden = jax.nn.gelu(
        hidden + expand_bias.astype(jnp.float32)[None, :, None, :], approximate=False
    ).astype(jnp.bfloat16)
    output = jnp.einsum("cisf,ifd->cisd", hidden, reduce_weight, preferred_element_type=jnp.float32)
    return (output + reduce_bias.astype(jnp.float32)[None, :, None, :]).astype(jnp.bfloat16)


def local(tokens, scales, slot_params, expand_weight, expand_bias, reduce_weight, reduce_bias):
    clip_count = lax.axis_size("clip")
    shard_count = lax.axis_size("shard")
    quantized = tokens[0]
    token_count, feature_dim = quantized.shape
    block_count = scales.shape[1]
    slot_count = slot_params.shape[1]
    owner_rows = slot_count // (clip_count * shard_count)
    experts_here = expand_weight.shape[0]
    slots_each = owner_rows // experts_here
    features = (
        quantized.reshape(token_count, block_count, feature_dim // block_count).astype(jnp.float32)
        * scales[0].T[:, :, None]
    )
    features = features.reshape(token_count, feature_dim).astype(jnp.bfloat16)
    logits = jnp.dot(features, slot_params, preferred_element_type=jnp.float32)
    row_peak = jnp.max(logits, axis=1, keepdims=True)
    row_weights = jnp.exp(logits - row_peak)
    combine_weight = (row_weights / jnp.sum(row_weights, axis=1, keepdims=True)).astype(
        jnp.bfloat16
    )
    column_peak = lax.pmax(jnp.max(logits, axis=0), "shard")
    column_total = lax.psum(jnp.sum(jnp.exp(logits - column_peak), axis=0), "shard")
    dispatch = (jnp.exp(logits - column_peak) / column_total).astype(jnp.bfloat16)
    partial_value = lax.dot_general(
        dispatch, features, (((0,), (0,)), ((), ())), preferred_element_type=jnp.float32
    )
    arrived = lax.all_to_all(
        partial_value, ("clip", "shard"), split_axis=0, concat_axis=0, tiled=True
    )
    slot_inputs = jnp.sum(
        arrived.reshape(clip_count, shard_count, owner_rows, feature_dim), axis=1
    ).astype(jnp.bfloat16)
    slot_outputs = expert_apply(
        slot_inputs.reshape(clip_count, experts_here, slots_each, feature_dim),
        expand_weight,
        expand_bias,
        reduce_weight,
        reduce_bias,
    )
    gathered = lax.all_gather(
        slot_outputs.reshape(1, clip_count * owner_rows, feature_dim), "shard", axis=0, tiled=True
    )
    returned = lax.all_to_all(gathered, "clip", split_axis=1, concat_axis=0, tiled=True)
    mixed = jnp.dot(
        combine_weight,
        returned.reshape(slot_count, feature_dim),
        preferred_element_type=jnp.float32,
    ).astype(jnp.bfloat16)
    return mixed[None]


def solution(mesh):
    placed = (
        P("clip", "shard", None),
        P("clip", None, "shard"),
        P(),
        P(("clip", "shard"), None, None),
        P(("clip", "shard"), None),
        P(("clip", "shard"), None, None),
        P(("clip", "shard"), None),
    )
    return jax.shard_map(
        local, mesh=mesh, in_specs=placed, out_specs=P("clip", "shard", None), check_vma=False
    )
```

profile of v0, /device:TPU:0, one launch (start us, length us, event | category | flops | bytes accessed | tf_op | source)
XLA Modules:
  0.0 90.1 jit_solution(5664969865137726673)
XLA Ops:
  0.0 0.9 copy.50
  0.9 5.7 %copy.30 = bf16[1,2304,768]{1,2,0:T(8,128)(2,1)} copy(bf16[1,2304,768]{2,1,0:T(8,128)(2,1)} %param.7) | data formatting | bytes 7077888 | tf_op args[0]
  6.6 2.8 %fusion.4 = bf16[2304,768]{0,1:T(8,128)(2,1)S(1)} fusion(f32[2304,6]{0,1:T(8,128)S(1)} %bitcast.124, bf16[1,2304,768]{1,2,0:T(8,128)(2,1)} %copy.30), kind=kLoop, calls=%fused_computation.5 | loop fusion | flops 5308416 | bytes 7133184 | tf_op jit(solution)/shard_map/convert_element_type | solution.py:36
  9.4 0.3 copy-done.1
  9.7 2.4 %multiply_convert_fusion = bf16[2304,6,128]{0,2,1:T(8,128)(2,1)} fusion(f32[2304,6]{0,1:T(8,128)S(1)} %bitcast.125, bf16[2304,6,128]{0,2,1:T(8,128)(2,1)S(1)} %bitcast.118), kind=kLoop, calls=%fused_computation.6 | loop fusion | flops 5308416 | bytes 7133184 | tf_op jit(solution)/shard_map/convert_element_type | solution.py:36
  12.1 0.8 fusion.46
  12.9 13.5 %pmax.7 = f32[128]{0:T(128)S(1)} all-reduce(f32[128]{0:T(128)S(1)} %get-tuple-element.8), channel_id=1, replica_groups=mesh['clip'=8,'shard'=4] {'shard'}, use_global_device_ids=true, to_apply=%region_3.0 | all-reduce | flops 128 | bytes 1024 | tf_op jit(solution)/shard_map/pmax | solution.py:43
  26.4 0.4 fusion.18
  26.8 8.4 %psum.7 = f32[128]{0:T(128)S(1)} all-reduce(f32[128]{0:T(128)S(1)} %get-tuple-element.6), channel_id=1, replica_groups=mesh['clip'=8,'shard'=4] {'shard'}, use_global_device_ids=true, to_apply=%region_5.0 | all-reduce | flops 128 | bytes 1024 | tf_op jit(solution)/shard_map/psum | solution.py:44
  35.1 0.3 fusion.24
  35.5 0.1 dot_general.18
  35.6 3.3 %fusion.20 = f32[32,4,768]{2,0,1:T(8,128)S(1)} fusion(bf16[2304,768,1]{0,1,2:T(8,128)(2,1)} %bitcast.121, bf16[32,4,2304]{2,1,0:T(4,128)(2,1)S(1)} %dot_general.18), kind=kOutput, calls=%fused_computation.20 | convolution fusion | flops 452984832 | bytes 4521984 | tf_op jit(solution)/shard_map/dot_general | solution.py:46
  38.9 1.0 %copy.33 = f32[32,4,768]{2,1,0:T(4,128)} copy(f32[32,4,768]{2,0,1:T(8,128)S(1)} %fusion.20) | data formatting | bytes 786432 | tf_op jit(solution)/shard_map/dot_general | solution.py:46
  39.9 4.2 %all-to-all-start = ((f32[32,4,768]{2,1,0:T(4,128)}), f32[32,4,768]{2,1,0:T(4,128)S(1)}, u32[]{:S(2)}, u32[]{:S(2)}) async-start(f32[32,4,768]{2,1,0:T(4,128)} %copy.33), calls=%async_computation | async-start | bytes 786432 | tf_op jit(solution)/shard_map/all_to_all | solution.py:49
  44.2 11.8 %all-to-all-done = f32[32,4,768]{2,1,0:T(4,128)S(1)} async-done(((f32[32,4,768]{2,1,0:T(4,128)}), f32[32,4,768]{2,1,0:T(4,128)S(1)}, u32[]{:S(2)}, u32[]{:S(2)}) %all-to-all-start) | async-done | bytes 393248 | tf_op jit(solution)/shard_map/all_to_all | solution.py:49
  56.1 0.1 multiply_reduce_fusion
  56.2 0.1 copy.34
  56.3 5.8 %fusion.27 = bf16[8,2,2,3072]{3,0,2,1:T(8,128)(2,1)S(1)} fusion(bf16[2,768,3072]{2,1,0:T(8,128)(2,1)} %param.10, f32[2,3072]{1,0:T(2,128)S(1)} %convert_element_type.94, f32[8,2,2,768]{3,0,2,1:T(8,128)S(1)} %bitcast.126, f32[8,2,2]{0,2,1:T(2,128)S(1)} %bitcast.127), kind=kOutput, calls=%fused_computation.27 | convolution fusion | flops 157532160 | bytes 9756800 | tf_op jit(solution)/shard_map/cisd,idf->cisf/dot_general | solution.py:12
  62.1 0.4 slice-done.2
  62.5 1.3 %fusion.15 = bf16[8,2,2,768]{3,0,2,1:T(8,128)(2,1)S(1)} fusion(bf16[8,2,2,3072]{3,0,2,1:T(8,128)(2,1)S(1)} %fusion.27, bf16[2,3072,768]{2,1,0:T(8,128)(2,1)S(1)} %bitcast.120, f32[2,768]{1,0:T(2,128)S(1)} %convert_element_type.96), kind=kOutput, calls=%fused_computation.16 | convolution fusion | flops 151044096 | bytes 9689088 | tf_op jit(solution)/shard_map/cisf,ifd->cisd/dot_general | solution.py:18
  63.9 13.9 %all_gather.3 = bf16[4,32,768]{2,1,0:T(8,128)(2,1)S(1)} all-gather(bf16[1,32,768]{2,1,0:T(8,128)(2,1)S(1)} %reshape.65), channel_id=1, replica_groups=mesh['clip'=8,'shard'=4] {'shard'}, dimensions={0}, use_global_device_ids=true | all-gather | bytes 245760 | tf_op jit(solution)/shard_map/all_gather | solution.py:62
  77.8 0.2 copy.37
  78.0 9.0 %all_to_all.21 = bf16[4,32,768]{2,0,1:T(4,128)(2,1)S(1)} all-to-all(bf16[4,32,768]{2,0,1:T(4,128)(2,1)S(1)} %copy.37), channel_id=1, replica_groups=mesh['clip'=8,'shard'=4] {'clip'}, dimensions={1} | all-to-all | bytes 393216 | tf_op jit(solution)/shard_map/all_to_all | solution.py:65
  87.1 2.9 %fusion.5 = bf16[1,2304,768]{2,1,0:T(8,128)(2,1)} fusion(bf16[128,768]{1,0:T(8,128)(2,1)S(1)} %reshape.66, f32[2304,128]{0,1:T(8,128)S(1)} %get-tuple-element.9, f32[2304]{0:T(1024)S(1)} %get-tuple-element.5, f32[2304]{0:T(1024)S(1)} %get-tuple-element.7), kind=kOutput, calls=%fused_computation.8 | convolution fusion | flops 455639040 | bytes 4933632 | tf_op jit(solution)/shard_map/dot_general | solution.py:66
  (22 shorter events, 0.3 us)
Async XLA Ops:
  0.0 12.1 %copy-start = (bf16[768,128]{1,0:T(8,128)(2,1)S(1)}, bf16[768,128]{1,0:T(8,128)(2,1)}, u32[]{:S(2)}) copy-start(bf16[768,128]{1,0:T(8,128)(2,1)} %param.9) | copy-start | bytes 589828
  6.6 3.1 %copy-start.1 = (bf16[1,2304,768]{1,2,0:T(8,128)(2,1)S(1)}, bf16[1,2304,768]{1,2,0:T(8,128)(2,1)}, u32[]{:S(2)}) copy-start(bf16[1,2304,768]{1,2,0:T(8,128)(2,1)} %copy.30) | copy-start | bytes 10616836
  35.5 8.7 %copy-start.2 = (bf16[2,3072]{1,0:T(2,128)(2,1)S(1)}, bf16[2,3072]{1,0:T(2,128)(2,1)}, u32[]{:S(2)}) copy-start(bf16[2,3072]{1,0:T(2,128)(2,1)} %param.11) | copy-start | bytes 36868
  35.5 8.7 %copy-start.3 = (bf16[2,768]{1,0:T(2,128)(2,1)S(1)}, bf16[2,768]{1,0:T(2,128)(2,1)}, u32[]{:S(2)}) copy-start(bf16[2,768]{1,0:T(2,128)(2,1)} %param.13) | copy-start | bytes 9220
  39.9 16.1 %all-to-all-start = ((f32[32,4,768]{2,1,0:T(4,128)}), f32[32,4,768]{2,1,0:T(4,128)S(1)}, u32[]{:S(2)}, u32[]{:S(2)}) async-start(f32[32,4,768]{2,1,0:T(4,128)} %copy.33), calls=%async_computation | async-start | bytes 786432 | tf_op jit(solution)/shard_map/all_to_all | solution.py:49
  56.0 6.0 %slice-start = ((s8[9437184]{0:T(1024)(128)(4,1)}), s8[1048576]{0:T(1024)(128)(4,1)S(1)}, s32[]{:S(2)}) async-start(s8[9437184]{0:T(1024)(128)(4,1)} %bitcast.119), calls=%async_computation.2 | async-start | bytes 2097152
  56.3 5.8 %slice-start.1 = ((s8[9437184]{0:T(1024)(128)(4,1)}), s8[4194304]{0:T(1024)(128)(4,1)S(1)}, s32[]{:S(2)}) async-start(s8[9437184]{0:T(1024)(128)(4,1)} %bitcast.119), calls=%async_computation.3 | async-start | bytes 8388608
  56.3 6.2 %slice-start.2 = ((s8[9437184]{0:T(1024)(128)(4,1)}), s8[4194304]{0:T(1024)(128)(4,1)S(1)}, s32[]{:S(2)}) async-start(s8[9437184]{0:T(1024)(128)(4,1)} %bitcast.119), calls=%async_computation.4 | async-start | bytes 8388608
where the time goes:
time: 90.5 us; the launch traced here: 90.1 us
  blocking collectives  44.7 us (49%)
  matrix products  14.1 us (16%)
  waiting for transfers between devices  11.8 us (13%)
  local copies, waits for them, and re-layouts  8.94 us (10%)
  other arithmetic  6.13 us (7%)
  starting transfers between devices  4.25 us (5%)
    all_gather x1, blocking collectives, local(): lax.all_gather(slot_outputs.reshape(1, clip_count * owner_rows, feature_d...  13.9 us
    pmax x1, blocking collectives, local(): column_peak = lax.pmax(jnp.max(logits, axis=0), 'shard')  13.5 us
    all_to_all x1, waiting for transfers between devices, local(): lax.all_to_all(partial_value, ('clip', 'shard'), split_axis=0, concat_axi...  11.8 us
    all_to_all x1, blocking collectives, local(): lax.all_to_all(gathered, 'clip', split_axis=1, concat_axis=0, tiled=True)  9.01 us
    psum x1, blocking collectives, local(): lax.psum(jnp.sum(jnp.exp(logits - column_peak), axis=0), 'shard')  8.37 us
    unnamed x16, local copies, waits for them, and re-layouts  7.36 us
    dot_general x1, matrix products, expert_apply(): jnp.einsum('cisd,idf->cisf', normalized, expand_weight, preferred_element...  5.76 us
    convert_element_type x2, other arithmetic, local(): features = features.reshape(token_count, feature_dim).astype(jnp.bfloat16)  5.22 us
  transfers between devices with their start and end apart: 1, of which 1 were waited for; matrix products, arithmetic and copies ran while one was open for 0% of the time, Pallas kernels for 0%

commit v1 on v0

--- a/solution.py
+++ b/solution.py
@@ -41,7 +41,9 @@
         jnp.bfloat16
     )
     column_peak = lax.pmax(jnp.max(logits, axis=0), "shard")
-    column_total = lax.psum(jnp.sum(jnp.exp(logits - column_peak), axis=0), "shard")
+    column_total = jnp.sum(
+        lax.all_gather(jnp.sum(jnp.exp(logits - column_peak), axis=0), "shard"), axis=0
+    )
     dispatch = (jnp.exp(logits - column_peak) / column_total).astype(jnp.bfloat16)
     partial_value = lax.dot_general(
         dispatch, features, (((0,), (0,)), ((), ())), preferred_element_type=jnp.float32

time: 90.5 us -> 89.6 us (0.990)
    psum x1 -> x0, blocking collectives: 8.37 us -> none  [local(): lax.psum(jnp.sum(jnp.exp(logits - column_peak), axis=0), 'shard')]
    all_gather x0 -> x1, blocking collectives: none -> 7.51 us  [local(): lax.all_gather(jnp.sum(jnp.exp(logits - column_peak), axis=0), 'shard')]
where the time goes in v1:
time: 89.6 us; the launch traced here: 89.2 us
  blocking collectives  43.9 us (49%)
  matrix products  14.1 us (16%)
  waiting for transfers between devices  11.8 us (13%)
  local copies, waits for them, and re-layouts  8.94 us (10%)
  other arithmetic  6.15 us (7%)
  starting transfers between devices  4.27 us (5%)
    all_gather x1, blocking collectives, local(): lax.all_gather(slot_outputs.reshape(1, clip_count * owner_rows, feature_d...  13.9 us
    pmax x1, blocking collectives, local(): column_peak = lax.pmax(jnp.max(logits, axis=0), 'shard')  13.5 us
    all_to_all x1, waiting for transfers between devices, local(): lax.all_to_all(partial_value, ('clip', 'shard'), split_axis=0, concat_axi...  11.8 us
    all_to_all x1, blocking collectives, local(): lax.all_to_all(gathered, 'clip', split_axis=1, concat_axis=0, tiled=True)  9.01 us
    all_gather x1, blocking collectives, local(): lax.all_gather(jnp.sum(jnp.exp(logits - column_peak), axis=0), 'shard')  7.51 us
    unnamed x16, local copies, waits for them, and re-layouts  7.36 us
    dot_general x1, matrix products, expert_apply(): jnp.einsum('cisd,idf->cisf', normalized, expand_weight, preferred_element...  5.76 us
    convert_element_type x2, other arithmetic, local(): features = features.reshape(token_count, feature_dim).astype(jnp.bfloat16)  5.22 us
  transfers between devices with their start and end apart: 1, of which 1 were waited for; matrix products, arithmetic and copies ran while one was open for 0% of the time, Pallas kernels for 0%

profile of v1, /device:TPU:0, one launch (start us, length us, event | category | flops | bytes accessed | tf_op | source)
XLA Modules:
  0.0 89.2 jit_solution(8870576087857914763)
XLA Ops:
  0.0 0.9 copy.50
  0.9 5.7 %copy.30 = bf16[1,2304,768]{1,2,0:T(8,128)(2,1)} copy(bf16[1,2304,768]{2,1,0:T(8,128)(2,1)} %param.7) | data formatting | bytes 7077888 | tf_op args[0]
  6.6 2.8 %fusion.4 = bf16[2304,768]{0,1:T(8,128)(2,1)S(1)} fusion(f32[2304,6]{0,1:T(8,128)S(1)} %bitcast.125, bf16[1,2304,768]{1,2,0:T(8,128)(2,1)} %copy.30), kind=kLoop, calls=%fused_computation.5 | loop fusion | flops 5308416 | bytes 7133184 | tf_op jit(solution)/shard_map/convert_element_type | solution.py:36
  9.4 0.3 copy-done.1
  9.7 2.4 %multiply_convert_fusion = bf16[2304,6,128]{0,2,1:T(8,128)(2,1)} fusion(f32[2304,6]{0,1:T(8,128)S(1)} %bitcast.126, bf16[2304,6,128]{0,2,1:T(8,128)(2,1)S(1)} %bitcast.119), kind=kLoop, calls=%fused_computation.6 | loop fusion | flops 5308416 | bytes 7133184 | tf_op jit(solution)/shard_map/convert_element_type | solution.py:36
  12.1 0.8 fusion.46
  12.9 13.5 %pmax.7 = f32[128]{0:T(128)S(1)} all-reduce(f32[128]{0:T(128)S(1)} %get-tuple-element.8), channel_id=1, replica_groups=mesh['clip'=8,'shard'=4] {'shard'}, use_global_device_ids=true, to_apply=%region_3.0 | all-reduce | flops 128 | bytes 1024 | tf_op jit(solution)/shard_map/pmax | solution.py:43
  26.4 0.4 fusion.18
  26.8 7.5 %all-gather.1 = f32[4,1,128]{2,1,0:T(1,128)S(1)} all-gather(f32[1,1,128]{2,1,0:T(1,128)S(1)} %bitcast.128), channel_id=2, replica_groups=mesh['clip'=8,'shard'=4] {'shard'}, dimensions={0}, use_global_device_ids=true | all-gather | bytes 2560 | tf_op jit(solution)/shard_map/all_gather | solution.py:45
  34.3 0.3 fusion.24
  34.6 0.1 dot_general.18
  34.8 3.3 %fusion.20 = f32[32,4,768]{2,0,1:T(8,128)S(1)} fusion(bf16[2304,768,1]{0,1,2:T(8,128)(2,1)} %bitcast.122, bf16[32,4,2304]{2,1,0:T(4,128)(2,1)S(1)} %dot_general.18), kind=kOutput, calls=%fused_computation.20 | convolution fusion | flops 452984832 | bytes 4521984 | tf_op jit(solution)/shard_map/dot_general | solution.py:48
  38.1 1.0 %copy.33 = f32[32,4,768]{2,1,0:T(4,128)} copy(f32[32,4,768]{2,0,1:T(8,128)S(1)} %fusion.20) | data formatting | bytes 786432 | tf_op jit(solution)/shard_map/dot_general | solution.py:48
  39.1 4.3 %all-to-all-start = ((f32[32,4,768]{2,1,0:T(4,128)}), f32[32,4,768]{2,1,0:T(4,128)S(1)}, u32[]{:S(2)}, u32[]{:S(2)}) async-start(f32[32,4,768]{2,1,0:T(4,128)} %copy.33), calls=%async_computation | async-start | bytes 786432 | tf_op jit(solution)/shard_map/all_to_all | solution.py:51
  43.4 11.8 %all-to-all-done = f32[32,4,768]{2,1,0:T(4,128)S(1)} async-done(((f32[32,4,768]{2,1,0:T(4,128)}), f32[32,4,768]{2,1,0:T(4,128)S(1)}, u32[]{:S(2)}, u32[]{:S(2)}) %all-to-all-start) | async-done | bytes 393248 | tf_op jit(solution)/shard_map/all_to_all | solution.py:51
  55.3 0.1 multiply_reduce_fusion
  55.4 0.1 copy.34
  55.5 5.8 %fusion.27 = bf16[8,2,2,3072]{3,0,2,1:T(8,128)(2,1)S(1)} fusion(bf16[2,768,3072]{2,1,0:T(8,128)(2,1)} %param.10, f32[2,3072]{1,0:T(2,128)S(1)} %convert_element_type.94, f32[8,2,2,768]{3,0,2,1:T(8,128)S(1)} %bitcast.127, f32[8,2,2]{0,2,1:T(2,128)S(1)} %bitcast.129), kind=kOutput, calls=%fused_computation.27 | convolution fusion | flops 157532160 | bytes 9756800 | tf_op jit(solution)/shard_map/cisd,idf->cisf/dot_general | solution.py:12
  61.3 0.4 slice-done.2
  61.7 1.3 %fusion.15 = bf16[8,2,2,768]{3,0,2,1:T(8,128)(2,1)S(1)} fusion(bf16[8,2,2,3072]{3,0,2,1:T(8,128)(2,1)S(1)} %fusion.27, bf16[2,3072,768]{2,1,0:T(8,128)(2,1)S(1)} %bitcast.121, f32[2,768]{1,0:T(2,128)S(1)} %convert_element_type.96), kind=kOutput, calls=%fused_computation.16 | convolution fusion | flops 151044096 | bytes 9689088 | tf_op jit(solution)/shard_map/cisf,ifd->cisd/dot_general | solution.py:18
  63.1 13.9 %all_gather.11 = bf16[4,32,768]{2,1,0:T(8,128)(2,1)S(1)} all-gather(bf16[1,32,768]{2,1,0:T(8,128)(2,1)S(1)} %reshape.65), channel_id=1, replica_groups=mesh['clip'=8,'shard'=4] {'shard'}, dimensions={0}, use_global_device_ids=true | all-gather | bytes 245760 | tf_op jit(solution)/shard_map/all_gather | solution.py:64
  77.0 0.2 copy.37
  77.2 9.0 %all_to_all.21 = bf16[4,32,768]{2,0,1:T(4,128)(2,1)S(1)} all-to-all(bf16[4,32,768]{2,0,1:T(4,128)(2,1)S(1)} %copy.37), channel_id=1, replica_groups=mesh['clip'=8,'shard'=4] {'clip'}, dimensions={1} | all-to-all | bytes 393216 | tf_op jit(solution)/shard_map/all_to_all | solution.py:67
  86.3 2.9 %fusion.5 = bf16[1,2304,768]{2,1,0:T(8,128)(2,1)} fusion(bf16[128,768]{1,0:T(8,128)(2,1)S(1)} %reshape.66, f32[2304,128]{0,1:T(8,128)S(1)} %get-tuple-element.9, f32[2304]{0:T(1024)S(1)} %get-tuple-element.5, f32[2304]{0:T(1024)S(1)} %get-tuple-element.7), kind=kOutput, calls=%fused_computation.8 | convolution fusion | flops 455639040 | bytes 4933632 | tf_op jit(solution)/shard_map/dot_general | solution.py:68
  (23 shorter events, 0.3 us)
Async XLA Ops:
  0.0 12.1 %copy-start = (bf16[768,128]{1,0:T(8,128)(2,1)S(1)}, bf16[768,128]{1,0:T(8,128)(2,1)}, u32[]{:S(2)}) copy-start(bf16[768,128]{1,0:T(8,128)(2,1)} %param.9) | copy-start | bytes 589828
  6.6 3.1 %copy-start.1 = (bf16[1,2304,768]{1,2,0:T(8,128)(2,1)S(1)}, bf16[1,2304,768]{1,2,0:T(8,128)(2,1)}, u32[]{:S(2)}) copy-start(bf16[1,2304,768]{1,2,0:T(8,128)(2,1)} %copy.30) | copy-start | bytes 10616836
  34.6 8.7 %copy-start.2 = (bf16[2,3072]{1,0:T(2,128)(2,1)S(1)}, bf16[2,3072]{1,0:T(2,128)(2,1)}, u32[]{:S(2)}) copy-start(bf16[2,3072]{1,0:T(2,128)(2,1)} %param.11) | copy-start | bytes 36868
  34.6 8.8 %copy-start.3 = (bf16[2,768]{1,0:T(2,128)(2,1)S(1)}, bf16[2,768]{1,0:T(2,128)(2,1)}, u32[]{:S(2)}) copy-start(bf16[2,768]{1,0:T(2,128)(2,1)} %param.13) | copy-start | bytes 9220
  39.1 16.1 %all-to-all-start = ((f32[32,4,768]{2,1,0:T(4,128)}), f32[32,4,768]{2,1,0:T(4,128)S(1)}, u32[]{:S(2)}, u32[]{:S(2)}) async-start(f32[32,4,768]{2,1,0:T(4,128)} %copy.33), calls=%async_computation | async-start | bytes 786432 | tf_op jit(solution)/shard_map/all_to_all | solution.py:51
  55.2 6.0 %slice-start = ((s8[9437184]{0:T(1024)(128)(4,1)}), s8[1048576]{0:T(1024)(128)(4,1)S(1)}, s32[]{:S(2)}) async-start(s8[9437184]{0:T(1024)(128)(4,1)} %bitcast.120), calls=%async_computation.2 | async-start | bytes 2097152
  55.5 5.8 %slice-start.1 = ((s8[9437184]{0:T(1024)(128)(4,1)}), s8[4194304]{0:T(1024)(128)(4,1)S(1)}, s32[]{:S(2)}) async-start(s8[9437184]{0:T(1024)(128)(4,1)} %bitcast.120), calls=%async_computation.3 | async-start | bytes 8388608
  55.5 6.2 %slice-start.2 = ((s8[9437184]{0:T(1024)(128)(4,1)}), s8[4194304]{0:T(1024)(128)(4,1)S(1)}, s32[]{:S(2)}) async-start(s8[9437184]{0:T(1024)(128)(4,1)} %bitcast.120), calls=%async_computation.4 | async-start | bytes 8388608
